TPU v7x, 32 devices: a whole 2x2x4 slice. The times are simulated.
32 devices in a mesh: grp: 4 (over z), pen: 8 (over y, x, core).
Axes of the slice: x: 2, y: 2, z: 4, core: 2. Of those that a mesh axis runs over, the one named last changes fastest.
Arguments:
- cell_offsets: int32 [2, 1048576], P(None, ('grp', 'pen')), may hold values from 0 to 1
- cell_z: int32 [1048576], P(('grp', 'pen')), may hold values from 0 to 255
- frac: float32 [3, 1048576], P(None, ('grp', 'pen')), may hold values from 0 to 1
- charges: float32 [1048576], P(('grp', 'pen')), may hold values from -4 to 4
- tile_counts: int32 [16384], P(('grp', 'pen')), may hold values from 16 to 64, as said below
Outputs:
- forces: float32 [3, 1048576], P(None, ('grp', 'pen'))
- energy: float32 [], replicated
Inputs may be any that keep to these rules, and one draw needn't show every extreme that they name: `tile_counts`: live slots of each tile; some tile holds 64.
All inputs are finite; a program needn't handle non-finite values.
Results may differ from a plain program's by a relative error of at most 0.0003.
Values sent between devices are 32-bit elements; how exact they have to be, the bound alone decides.
A program may use at most 256 MiB of HBM per device.

v0:
```python
import math

import jax
import jax.numpy as jnp
from jax import lax
from jax.sharding import PartitionSpec as P

KX = 256
KY = 256
KZ = 256
ATOMS = 1048576


ewald_split = 0.6
highest = lax.Precision.HIGHEST


def shifted(block, axis, distance):
    devices = range(lax.axis_size(axis))
    route = [((i - distance) % len(devices), i) for i in devices]
    return lax.ppermute(block, axis, route)


def spline_rows(fracs):
    values = [jnp.ones_like(fracs)]
    fifth = values
    for order in range(2, 7):
        nxt = []
        for j in range(order):
            term = jnp.zeros_like(fracs)
            if j >= 1:
                term = values[j - 1] * (fracs + order - 1 - j)
            if j <= order - 2:
                term = term + values[j] * (1.0 - fracs + j)
            nxt.append(term / (order - 1))
        if order == 5:
            fifth = nxt
        values = nxt
    slopes = []
    for j in range(6):
        term = jnp.zeros_like(fracs)
        if j >= 1:
            term = fifth[j - 1]
        if j <= 4:
            term = term - fifth[j]
        slopes.append(term)
    return (values, slopes)


def tile_weights(offsets, zcell, fracs, charge, counts, size_z):
    slots = charge.shape[-1]
    live = (jnp.arange(slots, dtype=jnp.int32) < counts[..., None]).astype(jnp.float32)
    live_q = charge * live
    theta_x, slope_x = spline_rows(fracs[0])
    theta_y, slope_y = spline_rows(fracs[1])
    theta_z, slope_z = spline_rows(fracs[2])
    footing = jnp.arange(8, dtype=jnp.int32)[:, None]
    cells = jnp.arange(size_z, dtype=jnp.int32)
    weight_x = 0.0
    grade_x = 0.0
    weight_y = 0.0
    grade_y = 0.0
    weight_z = 0.0
    grade_z = 0.0
    for j in range(6):
        hit_x = (footing == offsets[0][..., None, :] + j).astype(jnp.float32)
        hit_y = (footing == offsets[1][..., None, :] + j).astype(jnp.float32)
        hit_z = (cells == (zcell[..., :, None] + j) % size_z).astype(jnp.float32)
        weight_x = weight_x + theta_x[j][..., None, :] * hit_x
        grade_x = grade_x + slope_x[j][..., None, :] * hit_x
        weight_y = weight_y + theta_y[j][..., None, :] * hit_y
        grade_y = grade_y + slope_y[j][..., None, :] * hit_y
        weight_z = weight_z + theta_z[j][..., :, None] * hit_z
        grade_z = grade_z + slope_z[j][..., :, None] * hit_z
    return (weight_x, grade_x, weight_y, grade_y, weight_z, grade_z, live_q)


def modulus(index, length):
    coeffs = (1.0 / 120.0, 26.0 / 120.0, 66.0 / 120.0, 26.0 / 120.0, 1.0 / 120.0)
    real_part = 0.0
    imag_part = 0.0
    for j in range(5):
        angle = (index * j % length).astype(jnp.float32) * (2.0 * math.pi / length)
        real_part = real_part + coeffs[j] * jnp.cos(angle)
        imag_part = imag_part + coeffs[j] * jnp.sin(angle)
    return real_part * real_part + imag_part * imag_part


def influence(index_x, index_y, index_z):
    freq_x = jnp.where(2 * index_x < KX, index_x, index_x - KX).astype(jnp.float32) / KX
    freq_y = jnp.where(2 * index_y < KY, index_y, index_y - KY).astype(jnp.float32) / KY
    freq_z = jnp.where(2 * index_z < KZ, index_z, index_z - KZ).astype(jnp.float32) / KZ
    square = freq_x * freq_x + freq_y * freq_y + freq_z * freq_z
    safe = jnp.where(square > 0, square, 1.0)
    volume = float(KX * KY * KZ)
    value = jnp.exp(-math.pi**2 * safe / ewald_split**2) / (math.pi * volume * safe)
    value = value / (modulus(index_x, KX) * modulus(index_y, KY) * modulus(index_z, KZ))
    return jnp.where(square > 0, value, 0.0)


def dft_tables(length):
    index = jnp.arange(length, dtype=jnp.int32)
    angle = (index[:, None] * index[None, :] % length).astype(jnp.float32) * (
        2.0 * math.pi / length
    )
    return (jnp.cos(angle), jnp.sin(angle))


def z_slots(groups):
    planes = KZ // (2 * groups) + 1
    owner = jnp.arange(groups, dtype=jnp.int32)[:, None]
    within = jnp.arange(planes, dtype=jnp.int32)[None, :]
    ordinary = owner * (planes - 1) + within
    frequency = jnp.where(within < planes - 1, ordinary, jnp.where(owner == 0, KZ // 2, 0))
    plane_weight = jnp.where(
        within < planes - 1, jnp.where(frequency == 0, 1.0, 2.0), jnp.where(owner == 0, 1.0, 0.0)
    )
    frequency = frequency.reshape(-1)
    plane_weight = plane_weight.reshape(-1).astype(jnp.float32)
    position = jnp.arange(KZ, dtype=jnp.int32)
    angle = (frequency[:, None] * position[None, :] % KZ).astype(jnp.float32) * (2.0 * math.pi / KZ)
    usable = (plane_weight > 0).astype(jnp.float32)[:, None]
    return (planes, frequency, plane_weight, jnp.cos(angle) * usable, jnp.sin(angle) * usable)


def forward_complex(data, cos_table, sin_table, shape, axis):
    direct = jnp.dot(cos_table, data, precision=highest).reshape(shape)
    other = jnp.dot(sin_table, data, precision=highest).reshape(shape)
    real_part = jnp.take(direct, 0, axis=axis) + jnp.take(other, 1, axis=axis)
    imag_part = jnp.take(direct, 1, axis=axis) - jnp.take(other, 0, axis=axis)
    return (real_part, imag_part)


def inverse_complex(data, cos_table, sin_table, shape, axis):
    direct = jnp.dot(cos_table, data, precision=highest).reshape(shape)
    other = jnp.dot(sin_table, data, precision=highest).reshape(shape)
    real_part = jnp.take(direct, 0, axis=axis) - jnp.take(other, 1, axis=axis)
    imag_part = jnp.take(other, 0, axis=axis) + jnp.take(direct, 1, axis=axis)
    return (real_part, imag_part)


def spectrum_pen_first(grid, block_x, block_y):
    cos_x, sin_x = dft_tables(KX)
    cos_y, sin_y = dft_tables(KY)
    planes, frequency, plane_weight, cos_z, sin_z = z_slots(lax.axis_size("pen"))
    slot_total = cos_z.shape[0]
    lines = KY // lax.axis_size("grp")
    real_z = jnp.einsum("xyz,kz->ykx", grid, cos_z, precision=highest)
    imag_z = -jnp.einsum("xyz,kz->ykx", grid, sin_z, precision=highest)
    outgoing = jnp.stack([real_z, imag_z], axis=2).reshape(block_y, slot_total * 2 * block_x)
    columns = lax.all_to_all(outgoing, "pen", split_axis=1, concat_axis=0, tiled=True)
    real_y, imag_y = forward_complex(columns, cos_y, sin_y, (KY, planes, 2, block_x), 2)
    sectioned = jnp.transpose(jnp.stack([real_y, imag_y], axis=-1), (2, 0, 1, 3)).reshape(
        block_x, KY * planes * 2
    )
    rows = lax.all_to_all(sectioned, "grp", split_axis=1, concat_axis=0, tiled=True)
    real_x, imag_x = forward_complex(rows, cos_x, sin_x, (KX, lines, planes, 2), 3)
    first = lax.axis_index("pen") * planes
    index_x = jnp.arange(KX, dtype=jnp.int32)[:, None, None]
    index_y = lax.axis_index("grp") * lines + jnp.arange(lines, dtype=jnp.int32)[None, :, None]
    index_z = lax.dynamic_slice_in_dim(frequency, first, planes)[None, None, :]
    local_weight = lax.dynamic_slice_in_dim(plane_weight, first, planes)[None, None, :]
    kernel = influence(index_x, index_y, index_z)
    spectral = 0.5 * jnp.sum(local_weight * kernel * (real_x * real_x + imag_x * imag_x))
    scaled = jnp.stack([kernel * real_x, kernel * imag_x], axis=-1).reshape(KX, lines * planes * 2)
    real_b, imag_b = inverse_complex(scaled, cos_x, sin_x, (KX, lines, planes, 2), 3)
    returning = jnp.stack([real_b, imag_b], axis=-1).reshape(KX, lines * planes * 2)
    rows_home = lax.all_to_all(returning, "grp", split_axis=0, concat_axis=1, tiled=True)
    rows_home = jnp.transpose(rows_home.reshape(block_x, KY, planes, 2), (1, 2, 3, 0)).reshape(
        KY, planes * 2 * block_x
    )
    real_c, imag_c = inverse_complex(rows_home, cos_y, sin_y, (KY, planes, 2, block_x), 2)
    leaving = jnp.stack([real_c, imag_c], axis=2).reshape(KY, planes * 2 * block_x)
    home = lax.all_to_all(leaving, "pen", split_axis=0, concat_axis=1, tiled=True).reshape(
        block_y, slot_total, 2, block_x
    )
    potential = jnp.einsum(
        "ykx,kz->xyz", home[:, :, 0], plane_weight[:, None] * cos_z, precision=highest
    )
    potential = potential - jnp.einsum(
        "ykx,kz->xyz", home[:, :, 1], plane_weight[:, None] * sin_z, precision=highest
    )
    return (potential, spectral)


def place_tiles(spread, tiles_x, tiles_y):
    shaped = spread.reshape(tiles_x, tiles_y, 4, 2, 4, 2, KZ)
    total = 0.0
    for i in range(4):
        for j in range(4):
            part = jnp.transpose(shaped[:, :, i, :, j], (0, 2, 1, 3, 4)).reshape(
                2 * tiles_x, 2 * tiles_y, KZ
            )
            total = total + jnp.pad(part, ((2 * i, 6 - 2 * i), (2 * j, 6 - 2 * j), (0, 0)))
    return total


def gather_tiles(extended, tiles_x, tiles_y):
    blocks = []
    for i in range(4):
        members = []
        for j in range(4):
            part = extended[2 * i : 2 * i + 2 * tiles_x, 2 * j : 2 * j + 2 * tiles_y]
            part = part.reshape(tiles_x, 2, tiles_y, 2, KZ)
            members.append(jnp.transpose(part, (0, 2, 1, 3, 4)))
        blocks.append(jnp.stack(members, axis=3))
    return jnp.stack(blocks, axis=2).reshape(tiles_x, tiles_y, 64, KZ)


def local(cell_offsets, cell_z, frac, charges, tile_counts):
    block_x = KX // lax.axis_size("grp")
    block_y = KY // lax.axis_size("pen")
    tiles_x = block_x // 2
    tiles_y = block_y // 2
    slots = charges.shape[0] // (tiles_x * tiles_y)
    offsets = cell_offsets.reshape(2, tiles_x, tiles_y, slots)
    zcell = cell_z.reshape(tiles_x, tiles_y, slots)
    fracs = frac.reshape(3, tiles_x, tiles_y, slots)
    charge = charges.reshape(tiles_x, tiles_y, slots)
    counts = tile_counts.reshape(tiles_x, tiles_y)
    weight_x, grade_x, weight_y, grade_y, weight_z, grade_z, live_q = tile_weights(
        offsets, zcell, fracs, charge, counts, KZ
    )
    pair = weight_x[..., :, None, :] * weight_y[..., None, :, :] * live_q[..., None, None, :]
    pair = pair.reshape(tiles_x, tiles_y, 64, slots)
    spread = jnp.einsum("abfs,absz->abfz", pair, weight_z, precision=highest)
    padded = place_tiles(spread, tiles_x, tiles_y)
    rim_y = shifted(padded[: block_x + 5, block_y : block_y + 5], "pen", 1)
    merged = padded[: block_x + 5, :block_y].at[:, :5].add(rim_y)
    rim_x = shifted(merged[block_x : block_x + 5], "grp", 1)
    grid = merged[:block_x].at[:5].add(rim_x)
    potential, spectral = spectrum_pen_first(grid, block_x, block_y)
    upper = shifted(potential[:5], "grp", -1)
    ext_x = jnp.concatenate([potential, upper, jnp.zeros((1, block_y, KZ), jnp.float32)], axis=0)
    beside = shifted(ext_x[:, :5], "pen", -1)
    extended = jnp.concatenate(
        [ext_x, beside, jnp.zeros((block_x + 6, 1, KZ), jnp.float32)], axis=1
    )
    footing = gather_tiles(extended, tiles_x, tiles_y)
    main = jnp.einsum("abfz,absz->abfs", footing, weight_z, precision=highest).reshape(
        tiles_x, tiles_y, 8, 8, slots
    )
    tilt = jnp.einsum("abfz,absz->abfs", footing, grade_z, precision=highest).reshape(
        tiles_x, tiles_y, 8, 8, slots
    )
    force_x = -live_q * jnp.einsum(
        "abxs,abys,abxys->abs", grade_x, weight_y, main, precision=highest
    )
    force_y = -live_q * jnp.einsum(
        "abxs,abys,abxys->abs", weight_x, grade_y, main, precision=highest
    )
    force_z = -live_q * jnp.einsum(
        "abxs,abys,abxys->abs", weight_x, weight_y, tilt, precision=highest
    )
    total = lax.psum(spectral, ("grp", "pen"))
    forces = jnp.stack([force_x, force_y, force_z], axis=0).reshape(3, tiles_x * tiles_y * slots)
    return (forces, total / ATOMS)


def solution(mesh):
    in_specs = (
        P(None, ("grp", "pen")),
        P(("grp", "pen")),
        P(None, ("grp", "pen")),
        P(("grp", "pen")),
        P(("grp", "pen")),
    )
    out_specs = (P(None, ("grp", "pen")), P())
    return jax.shard_map(local, mesh=mesh, in_specs=in_specs, out_specs=out_specs, check_vma=False)
```

profile of v0, /device:TPU:0, one launch (start us, length us, event | category | flops | bytes accessed | tf_op | source)
XLA Modules:
  0.0 1139.1 jit_solution(11327651914012425456)
XLA Ops:
  23.0 140.8 %fusion.15 = f32[32,16,64,256]{3,2,1,0:T(8,128)} fusion(f32[32,16,64]{2,1,0:T(8,128)S(1)} %copy-done.60, s32[32,16,64]{2,1,0:T(8,128)S(1)} %get-tuple-element.184, f32[32,16,64]{2,1,0:T(8,128)S(1)} %copy-done.58, s32[32,16,64]{2,1,0:T(8,128)S(1)} %get-tuple-element.183, f32[32,16,64]{2,1,0:T(8,128)S(1)} %copy-done.54, ...), kind=kOutput, calls=%fused_computation.27 | convolution fusion | flops 6589251584 | bytes 37355520 | tf_op jit(solution)/shard_map/abfs,absz->abfz/dot_general | solution.py:226
  163.8 39.0 %reshape.1907 = f32[32,16,4,2,4,2,256]{6,5,4,3,2,1,0:T(2,128)} reshape(f32[32,16,64,256]{3,2,1,0:T(8,128)} %fusion.15) | data formatting | bytes 67108864 | tf_op jit(solution)/shard_map/reshape | solution.py:187
  202.8 25.3 %slice_bitcast_fusion.15 = (f32[32,2,16,2,256]{4,3,1,2,0:T(2,128)S(1)}, f32[32,2,16,2,256]{4,3,1,2,0:T(2,128)S(1)}, f32[32,2,16,2,256]{4,3,1,2,0:T(2,128)}, f32[...) fusion(f32[32,16,4,2,4,2,256]{6,5,4,3,2,1,0:T(2,128)} %reshape.1907), kind=kLoop, calls=%fused_computation.93 | loop fusion | bytes 67108864 | tf_op jit(solution)/shard_map/transpose | solution.py:191
  241.8 4.1 copy.276
  257.4 4.1 copy.278
  288.2 4.0 copy.282
  303.7 4.1 copy.284
  319.2 4.1 copy.286
  338.6 4.0 reshape.1922
  348.7 12.9 %pad_add_fusion = f32[70,38,256]{2,0,1:T(8,128)S(1)} fusion(f32[64,32,256]{2,0,1:T(8,128)} %reshape.1923, f32[64,32,256]{2,0,1:T(8,128)} %reshape.1922, f32[64,32,256]{2,0,1:T(8,128)} %reshape.1921, f32[64,32,256]{2,0,1:T(8,128)} %reshape.1920, f32[64,32,256]{2,0,1:T(8,128)} %reshape.1919, f32[64,32,256]{2,0,1:T(8,128)} %reshape.1918, ...), kind=kLoop, calls=%fused_computation.52 | loop fusion | flops 10214400 | bytes 36278272 | tf_op jit(solution)/shard_map/add | solution.py:194
  365.4 4.7 collective-permute-done
  376.0 5.0 collective-permute-done.1
  389.5 7.5 copy.290
  397.0 4.6 all_to_all.52
  402.1 31.3 %all_to_all.70 = f32[32,8,2176]{2,0,1:T(8,128)} all-to-all(f32[32,8,2176]{2,0,1:T(8,128)S(1)} %copy.291), channel_id=1, replica_groups=mesh['grp'=4,'pen'=8] {'pen'}, dimensions={1} | all-to-all | bytes 4456448 | tf_op jit(solution)/shard_map/all_to_all | solution.py:151
  442.0 5.1 copy.296
  447.1 5.1 copy.297
  456.6 50.4 %all-to-all-done.1 = f32[64,4,2176]{2,0,1:T(8,128)S(1)} async-done(((f32[64,4,2176]{2,0,1:T(8,128)}), f32[64,4,2176]{2,0,1:T(8,128)S(1)}, u32[]{:S(2)}, u32[]{:S(2)}) %all-to-all-start.1) | async-done | bytes 2228256 | tf_op jit(solution)/shard_map/all_to_all | solution.py:156
  535.7 4.9 all_to_all.60
  540.5 4.5 copy.311
  545.1 54.0 %all_to_all.71 = f32[4,64,2176]{2,1,0:T(8,128)} all-to-all(f32[4,64,2176]{2,1,0:T(8,128)S(1)} %copy.311), channel_id=1, replica_groups=mesh['grp'=4,'pen'=8] {'grp'}, dimensions={0} | all-to-all | bytes 4456448 | tf_op jit(solution)/shard_map/all_to_all | solution.py:168
  599.1 4.7 copy.312
  603.8 7.0 copy.372
  610.8 6.1 copy.313
  617.0 4.6 fusion.36
  625.2 5.1 copy.317
  630.3 4.6 all_to_all.63
  634.9 30.6 %all_to_all.72 = f32[8,32,2176]{2,1,0:T(8,128)S(1)} all-to-all(f32[8,32,2176]{2,1,0:T(8,128)S(1)} %all_to_all.63), channel_id=1, replica_groups=mesh['grp'=4,'pen'=8] {'pen'}, dimensions={0} | all-to-all | bytes 4456448 | tf_op jit(solution)/shard_map/all_to_all | solution.py:174
  666.9 4.1 reshape.1927
  671.0 8.8 fusion.280
  679.8 5.8 copy.378
  685.6 5.3 fusion.141
  690.9 4.7 copy.377
  695.6 4.2 fusion.143
  702.0 55.4 %select_add_fusion.1.clone.4 = f32[32,16,64,256]{3,2,1,0:T(8,128)} fusion(f32[32,16,64]{2,1,0:T(8,128)S(1)} %copy-done.61, s32[32,16,64]{2,1,0:T(8,128)S(1)} %copy-done.43, f32[32,16,64]{2,1,0:T(8,128)S(1)} %copy-done.59, s32[32,16,64]{2,1,0:T(8,128)S(1)} %copy-done.41, f32[32,16,64]{2,1,0:T(8,128)S(1)} %copy-done.55, ...), kind=kLoop, calls=%fused_computation.13.clone.clone.clone.clone.1 | loop fusion | flops 142606336 | bytes 35127296 | tf_op jit(solution)/shard_map/abxs,abys,abxys->abs/dot_general | solution.py:246
  758.8 55.3 %fusion.294 = f32[32,16,64,256]{3,2,1,0:T(8,128)} fusion(f32[32,16,64]{2,1,0:T(8,128)S(1)} %copy-done.53, f32[32,16,64]{2,1,0:T(8,128)S(1)} %copy-done.51, f32[32,16,64]{2,1,0:T(8,128)S(1)} %copy-done.50, f32[32,16,64]{2,1,0:T(8,128)S(1)} %copy-done.52, f32[32,16,64]{2,1,0:T(8,128)S(1)} %copy-done.49, f32[32,16,64]{2,1,0:T(8,128)S(1)} %copy-done.48, ...), kind=kLoop, calls=%fused_computation.2.clone.clone.clone.1 | loop fusion | flops 142606336 | bytes 35127296 | tf_op jit(solution)/shard_map/abfz,absz->abfs/dot_general | solution.py:243
  814.8 38.4 %psum.7 = f32[]{:T(128)} all-reduce(f32[]{:T(128)S(6)} %mul_shard_map.3), channel_id=1, replica_groups=mesh['grp'=4,'pen'=8] {'grp','pen'}, use_global_device_ids=true, to_apply=%region_1.6 | all-reduce | flops 1 | bytes 8 | tf_op jit(solution)/shard_map/psum | solution.py:255
  869.6 6.2 fusion.282
  916.5 6.8 maximum_bitcast_fusion
  923.3 4.5 maximum_bitcast_fusion.1
  927.9 5.3 maximum_bitcast_fusion.2
  934.2 5.2 maximum_bitcast_fusion.3
  939.5 18.5 %pad_maximum_fusion = f32[32,16,4,2,4,2,256]{6,3,0,5,1,4,2:T(2,128)} fusion(f32[32,16,1,2,4,2,256]{6,3,0,5,1,4,2:T(2,128)} %maximum_bitcast_fusion.3, f32[32,16,1,2,4,2,256]{6,3,0,5,1,4,2:T(2,128)} %maximum_bitcast_fusion.2, f32[32,16,1,2,4,2,256]{6,3,0,5,1,4,2:T(2,128)S(1)} %maximum_bitcast_fusion.1, f32[32,16,1,2,4,2,256]{6,3,0,5,1,4,2:T(2,128)S(1)} %maximum_bitcast_fusion), kind=kLoop, calls=%fused_computation | loop fusion | flops 25165824 | bytes 67108864 | tf_op jit(solution)/shard_map/stack | solution.py:207
  958.0 46.1 %copy.321 = f32[32,16,4,2,4,2,256]{6,5,4,3,2,1,0:T(2,128)} copy(f32[32,16,4,2,4,2,256]{6,3,0,5,1,4,2:T(2,128)} %pad_maximum_fusion) | data formatting | bytes 67108864 | tf_op jit(solution)/shard_map/stack | solution.py:207
  1004.1 39.9 %reshape.1944 = f32[32,16,64,256]{3,2,1,0:T(8,128)} reshape(f32[32,16,4,2,4,2,256]{6,5,4,3,2,1,0:T(2,128)} %copy.321) | data formatting | bytes 67108864 | tf_op jit(solution)/shard_map/reshape | solution.py:207
  1044.0 42.5 %fusion.12 = f32[32,16,64,8]{2,3,1,0:T(8,128)} fusion(f32[32,16,64,8]{2,3,1,0:T(8,128)S(1)} %bitcast.442, f32[32,16,64,256]{3,2,1,0:T(8,128)} %reshape.1944, f32[32,16,64,256]{3,2,1,0:T(8,128)} %fusion.294), kind=kOutput, calls=%fused_computation.21 | convolution fusion | flops 6446383104 | bytes 69206016 | tf_op jit(solution)/shard_map/abfz,absz->abfs/dot_general | solution.py:243
  1086.5 41.7 %fusion.13 = (f32[32,16,64,8]{2,3,1,0:T(8,128)}, f32[32,16,64,8]{2,3,1,0:T(8,128)}) fusion(f32[32,16,64,8]{2,3,1,0:T(8,128)} %get-tuple-element.128, f32[32,16,64,8]{2,3,1,0:T(8,128)S(1)} %bitcast.443, f32[32,16,64,256]{3,2,1,0:T(8,128)} %reshape.1944, f32[32,16,64,256]{3,2,1,0:T(8,128)} %select_add_fusion.1.clone.4), kind=kOutput, calls=%fused_computation.24 | convolution fusion | flops 6450315264 | bytes 71303168 | tf_op jit(solution)/shard_map/abfz,absz->abfs/dot_general | solution.py:240
  1128.3 4.9 multiply_reduce_fusion.2
  (327 shorter events, 248.2 us)
Async XLA Ops:
  13.3 8.3 copy-start.32
  13.3 8.3 copy-start.34
  13.3 8.3 copy-start.36
  13.3 8.3 copy-start.38
  13.4 8.3 copy-start.40
  13.4 8.3 copy-start.42
  13.5 4.3 copy-start.44
  13.6 4.3 copy-start.90
  13.8 4.1 copy-start.47
  13.8 4.1 copy-start.66
  18.0 4.9 copy-start.54
  18.0 4.9 copy-start.56
  18.0 4.9 copy-start.58
  18.1 4.9 copy-start.60
  18.1 4.9 copy-start.62
  18.1 4.9 copy-start.64
  361.6 8.5 collective-permute-start
  371.9 9.2 collective-permute-start.1
  452.2 54.8 %all-to-all-start.1 = ((f32[64,4,2176]{2,0,1:T(8,128)}), f32[64,4,2176]{2,0,1:T(8,128)S(1)}, u32[]{:S(2)}, u32[]{:S(2)}) async-start(f32[64,4,2176]{2,0,1:T(8,128)} %copy.297), calls=%async_computation.1 | async-start | bytes 4456448 | tf_op jit(solution)/shard_map/all_to_all | solution.py:156
  695.6 4.3 copy-start.6
  700.4 57.0 %collective-permute-start.2 = (f32[5,32,256]{2,0,1:T(8,128)S(1)}, f32[5,32,256]{2,0,1:T(8,128)S(1)}, u32[]{:S(2)}, u32[]{:S(2)}) collective-permute-start(f32[5,32,256]{2,0,1:T(8,128)S(1)} %slice.369), channel_id=1, source_target_pairs={{8,0},{16,8},{24,16},{0,24},{9,1},{17,9},{25,17},{1,25},{10,2},{18... | collective-permute-start | bytes 491528 | tf_op jit(solution)/shard_map/ppermute | solution.py:21
  757.5 111.8 %collective-permute-start.3 = (f32[70,5,256]{2,0,1:T(8,128)S(1)}, f32[70,5,256]{2,0,1:T(8,128)S(1)}, u32[]{:S(2)}, u32[]{:S(2)}) collective-permute-start(f32[70,5,256]{2,0,1:T(8,128)S(1)} %pad_maximum_fusion.10), channel_id=1, source_target_pairs={{1,0},{2,1},{3,2},{4,3},{5,4},{6,5},{7,6},{0,7},{9,8},{10,9},{11,1... | collective-permute-start | bytes 1075208 | tf_op jit(solution)/shard_map/ppermute | solution.py:21
  916.5 6.8 copy-start.10
  916.5 6.8 copy-start.11
  916.5 6.8 copy-start.12
  916.5 6.8 copy-start.14
  923.3 4.5 copy-start.8
  923.3 4.5 copy-start.13
  923.3 4.5 copy-start.15
  923.3 4.5 copy-start.17
  927.9 5.3 copy-start.7
  927.9 5.3 copy-start.16
  927.9 5.6 copy-start.18
  927.9 6.4 copy-start.19
  1004.1 39.9 %copy-start.1 = (f32[32,16,8,64]{3,2,1,0:T(8,128)S(1)}, f32[32,16,8,64]{3,2,1,0:T(8,128)}, u32[]{:S(2)}) copy-start(f32[32,16,8,64]{3,2,1,0:T(8,128)} %copy-done) | copy-start | bytes 3145732
  1086.4 41.7 %copy-start.21 = (s32[32,16,64]{2,1,0:T(8,128)S(1)}, s32[32,16,64]{2,1,0:T(8,128)}, u32[]{:S(2)}) copy-start(s32[32,16,64]{2,1,0:T(8,128)} %copy-done.20) | copy-start | bytes 393220
  1086.4 41.7 %copy-start.23 = (s32[32,16,64]{2,1,0:T(8,128)S(1)}, s32[32,16,64]{2,1,0:T(8,128)}, u32[]{:S(2)}) copy-start(s32[32,16,64]{2,1,0:T(8,128)} %copy-done.22) | copy-start | bytes 393220
  1086.4 41.7 %copy-start.25 = (s32[32,16,64]{2,1,0:T(8,128)S(1)}, s32[32,16,64]{2,1,0:T(8,128)}, u32[]{:S(2)}) copy-start(s32[32,16,64]{2,1,0:T(8,128)} %copy-done.24) | copy-start | bytes 393220
  1086.4 41.7 %copy-start.27 = (s32[32,16,64]{2,1,0:T(8,128)S(1)}, s32[32,16,64]{2,1,0:T(8,128)}, u32[]{:S(2)}) copy-start(s32[32,16,64]{2,1,0:T(8,128)} %copy-done.26) | copy-start | bytes 393220
  1086.4 41.7 %copy-start.29 = (s32[32,16,64]{2,1,0:T(8,128)S(1)}, s32[32,16,64]{2,1,0:T(8,128)}, u32[]{:S(2)}) copy-start(s32[32,16,64]{2,1,0:T(8,128)} %copy-done.28) | copy-start | bytes 393220
  1128.2 4.9 copy-start.4
  1128.2 4.9 copy-start.31
  1128.2 4.9 copy-start.83
  1128.2 4.9 copy-start.84
  1128.2 4.9 copy-start.85
  1128.2 4.9 copy-start.86
  1128.2 4.9 copy-start.87
  1128.2 4.9 copy-start.88
  (52 other events, 151.1 us)
where the time goes:
time: 1150 us; the launch traced here: 1140 us
  local copies, waits for them, and re-layouts  446 us (39%)
  matrix products  265 us (23%)
  other arithmetic  201 us (17%)
  blocking collectives  154 us (13%)
  waiting for transfers between devices  60.1 us (5%)
    dot_general x1, matrix products, local(): spread = jnp.einsum('abfs,absz->abfz', pair, weight_z, precision=highest)  141 us
    transpose x17, local copies, waits for them, and re-layouts, place_tiles(): jnp.transpose(shaped[:, :, i, :, j], (0, 2, 1, 3, 4))  86.3 us
    dot_general x2, other arithmetic, local(): jnp.einsum('abxs,abys,abxys->abs', grade_x, weight_y, main, precision=hig...  60.3 us
    reshape x16, local copies, waits for them, and re-layouts, place_tiles(): jnp.transpose(shaped[:, :, i, :, j], (0, 2, 1, 3, 4))  59.5 us
    dot_general x1, other arithmetic, local(): jnp.einsum('abfz,absz->abfs', footing, grade_z, precision=highest)  55.3 us
    all_to_all x1, blocking collectives, spectrum_pen_first(): lax.all_to_all(returning, 'grp', split_axis=0, concat_axis=1, tiled=True)  54 us
    all_to_all x1, waiting for transfers between devices, spectrum_pen_first(): lax.all_to_all(sectioned, 'grp', split_axis=1, concat_axis=0, tiled=True)  50.4 us
    reshape x16, local copies, waits for them, and re-layouts, gather_tiles(): part = part.reshape(tiles_x, 2, tiles_y, 2, KZ)  50 us
  transfers between devices with their start and end apart: 5, of which 3 were waited for; matrix products, arithmetic and copies ran while one was open for 12% of the time, Pallas kernels for 0%

commit v1 on v0

--- a/solution.py
+++ b/solution.py
@@ -1,8 +1,11 @@
+import functools
 import math
 
 import jax
 import jax.numpy as jnp
 from jax import lax
+from jax.experimental import pallas as pl
+from jax.experimental.pallas import tpu as pltpu
 from jax.sharding import PartitionSpec as P
 
 KX = 256
@@ -12,7 +15,7 @@
 
 
 ewald_split = 0.6
-highest = lax.Precision.HIGHEST
+highest = lax.Precision.HIGH
 
 
 def shifted(block, axis, distance):
@@ -47,32 +50,144 @@
     return (values, slopes)
 
 
-def tile_weights(offsets, zcell, fracs, charge, counts, size_z):
-    slots = charge.shape[-1]
-    live = (jnp.arange(slots, dtype=jnp.int32) < counts[..., None]).astype(jnp.float32)
-    live_q = charge * live
-    theta_x, slope_x = spline_rows(fracs[0])
-    theta_y, slope_y = spline_rows(fracs[1])
-    theta_z, slope_z = spline_rows(fracs[2])
-    footing = jnp.arange(8, dtype=jnp.int32)[:, None]
-    cells = jnp.arange(size_z, dtype=jnp.int32)
-    weight_x = 0.0
-    grade_x = 0.0
-    weight_y = 0.0
-    grade_y = 0.0
-    weight_z = 0.0
-    grade_z = 0.0
+def select_rows(distance, values):
+    total = jnp.zeros(distance.shape, jnp.float32)
     for j in range(6):
-        hit_x = (footing == offsets[0][..., None, :] + j).astype(jnp.float32)
-        hit_y = (footing == offsets[1][..., None, :] + j).astype(jnp.float32)
-        hit_z = (cells == (zcell[..., :, None] + j) % size_z).astype(jnp.float32)
-        weight_x = weight_x + theta_x[j][..., None, :] * hit_x
-        grade_x = grade_x + slope_x[j][..., None, :] * hit_x
-        weight_y = weight_y + theta_y[j][..., None, :] * hit_y
-        grade_y = grade_y + slope_y[j][..., None, :] * hit_y
-        weight_z = weight_z + theta_z[j][..., :, None] * hit_z
-        grade_z = grade_z + slope_z[j][..., :, None] * hit_z
-    return (weight_x, grade_x, weight_y, grade_y, weight_z, grade_z, live_q)
+        total = jnp.where(distance == j, values[j], total)
+    return total
+
+
+def select_pair(distance, values, grades):
+    total = jnp.zeros(distance.shape, jnp.float32)
+    slope = jnp.zeros(distance.shape, jnp.float32)
+    for j in range(6):
+        hit = distance == j
+        total = jnp.where(hit, values[j], total)
+        slope = jnp.where(hit, grades[j], slope)
+    return (total, slope)
+
+
+def split(values):
+    high = values.astype(jnp.bfloat16)
+    low = (values - high.astype(jnp.float32)).astype(jnp.bfloat16)
+    return (high, low)
+
+
+def product(high, low, other, dims):
+    other_high, other_low = split(other)
+    rows = high.shape[0]
+    both = lax.dot_general(
+        jnp.concatenate([high, low], axis=0), other_high, dims, preferred_element_type=jnp.float32
+    )
+    rest = lax.dot_general(high, other_low, dims, preferred_element_type=jnp.float32)
+    return both[:rows] + both[rows:] + rest
+
+
+def row_of(values, i):
+    return [value[i : i + 1] for value in values]
+
+
+def y_offset(offset, slots):
+    lane = lax.broadcasted_iota(jnp.int32, offset.shape, 1)
+    return offset + 2 * (lane // slots)
+
+
+def spread_kernel(per_row, slots, off_ref, z_ref, frac_ref, q_ref, grid_ref):
+    width = z_ref.shape[1]
+    size_z = grid_ref.shape[2]
+    grid_ref[...] = jnp.zeros_like(grid_ref)
+
+    def step(outer, carry):
+        rows = pl.ds(pl.multiple_of(outer * 8, 8), 8)
+        theta_x, _ = spline_rows(frac_ref[0, rows, :])
+        theta_y, _ = spline_rows(frac_ref[1, rows, :])
+        theta_z, _ = spline_rows(frac_ref[2, rows, :])
+        charge = q_ref[rows, :]
+        theta_x = [theta * charge for theta in theta_x]
+        off_x = off_ref[0, rows, :]
+        off_y = y_offset(off_ref[1, rows, :], slots)
+        base = z_ref[rows, :]
+        eight = lax.broadcasted_iota(jnp.int32, (8, width), 0)
+        sixteen = lax.broadcasted_iota(jnp.int32, (16, width), 0)
+        cells = lax.broadcasted_iota(jnp.int32, (size_z, width), 0)
+        for i in range(8):
+            weight_x = select_rows(eight - off_x[i : i + 1], row_of(theta_x, i))
+            weight_y = select_rows(sixteen - off_y[i : i + 1], row_of(theta_y, i))
+            weight_z = select_rows(
+                (cells - base[i : i + 1]) & (size_z - 1), row_of(theta_z, i)
+            )
+            pair = jnp.concatenate([weight_x[k : k + 1] * weight_y for k in range(8)], axis=0)
+            high, low = split(pair)
+            out = product(high, low, weight_z, (((1,), (1,)), ((), ())))
+            first = 2 * (outer * (8 // per_row) + i // per_row)
+            y0 = 8 * (i % per_row)
+            for k in range(8):
+                grid_ref[first + k, y0 : y0 + 16, :] += out[16 * k : 16 * k + 16]
+        return carry
+
+    lax.fori_loop(0, z_ref.shape[0] // 8, step, 0)
+
+
+def interp_kernel(
+    per_row, slots, off_ref, z_ref, frac_ref, q_ref, pot_ref, up_ref, side_ref, out_ref, ext_ref
+):
+    width = z_ref.shape[1]
+    size_z = pot_ref.shape[2]
+    block_x, block_y = pot_ref.shape[0], pot_ref.shape[1]
+    ext_ref[:block_x, :block_y] = pot_ref[...]
+    ext_ref[block_x : block_x + 5, :block_y] = up_ref[...]
+    ext_ref[block_x + 5 :, :block_y] = jnp.zeros((3, block_y, size_z), jnp.float32)
+    ext_ref[: block_x + 5, block_y:] = side_ref[...]
+    ext_ref[block_x + 5 :, block_y:] = jnp.zeros((3, 8, size_z), jnp.float32)
+
+    def step(outer, carry):
+        rows = pl.ds(pl.multiple_of(outer * 8, 8), 8)
+        theta_x, slope_x = spline_rows(frac_ref[0, rows, :])
+        theta_y, slope_y = spline_rows(frac_ref[1, rows, :])
+        theta_z, slope_z = spline_rows(frac_ref[2, rows, :])
+        off_x = off_ref[0, rows, :]
+        off_y = y_offset(off_ref[1, rows, :], slots)
+        base = z_ref[rows, :]
+        eight = lax.broadcasted_iota(jnp.int32, (8, width), 0)
+        sixteen = lax.broadcasted_iota(jnp.int32, (16, width), 0)
+        cells = lax.broadcasted_iota(jnp.int32, (size_z, width), 0)
+        dims = (((1,), (0,)), ((), ()))
+        forces = [[], [], []]
+        for i in range(8):
+            weight_x, grade_x = select_pair(
+                eight - off_x[i : i + 1], row_of(theta_x, i), row_of(slope_x, i)
+            )
+            weight_y, grade_y = select_pair(
+                sixteen - off_y[i : i + 1], row_of(theta_y, i), row_of(slope_y, i)
+            )
+            weight_z, grade_z = select_pair(
+                (cells - base[i : i + 1]) & (size_z - 1), row_of(theta_z, i), row_of(slope_z, i)
+            )
+            first = 2 * (outer * (8 // per_row) + i // per_row)
+            y0 = 8 * (i % per_row)
+            footing = jnp.concatenate(
+                [ext_ref[first + k, y0 : y0 + 16, :] for k in range(8)], axis=0
+            )
+            high, low = split(footing)
+            main = product(high, low, weight_z, dims)
+            tilt = product(high, low, grade_z, dims)
+            along_x = 0.0
+            along_y = 0.0
+            along_z = 0.0
+            for k in range(8):
+                piece = main[16 * k : 16 * k + 16]
+                along_x = along_x + grade_x[k : k + 1] * piece
+                along_y = along_y + weight_x[k : k + 1] * piece
+                along_z = along_z + weight_x[k : k + 1] * tilt[16 * k : 16 * k + 16]
+            forces[0].append(jnp.sum(along_x * weight_y, axis=0, keepdims=True))
+            forces[1].append(jnp.sum(along_y * grade_y, axis=0, keepdims=True))
+            forces[2].append(jnp.sum(along_z * weight_y, axis=0, keepdims=True))
+        minus_q = -q_ref[rows, :]
+        for d in range(3):
+            out_ref[d, rows, :] = minus_q * jnp.concatenate(forces[d], axis=0)
+        return carry
+
+    lax.fori_loop(0, z_ref.shape[0] // 8, step, 0)
 
 
 def modulus(index, length):
@@ -183,78 +298,49 @@
     return (potential, spectral)
 
 
-def place_tiles(spread, tiles_x, tiles_y):
-    shaped = spread.reshape(tiles_x, tiles_y, 4, 2, 4, 2, KZ)
-    total = 0.0
-    for i in range(4):
-        for j in range(4):
-            part = jnp.transpose(shaped[:, :, i, :, j], (0, 2, 1, 3, 4)).reshape(
-                2 * tiles_x, 2 * tiles_y, KZ
-            )
-            total = total + jnp.pad(part, ((2 * i, 6 - 2 * i), (2 * j, 6 - 2 * j), (0, 0)))
-    return total
-
-
-def gather_tiles(extended, tiles_x, tiles_y):
-    blocks = []
-    for i in range(4):
-        members = []
-        for j in range(4):
-            part = extended[2 * i : 2 * i + 2 * tiles_x, 2 * j : 2 * j + 2 * tiles_y]
-            part = part.reshape(tiles_x, 2, tiles_y, 2, KZ)
-            members.append(jnp.transpose(part, (0, 2, 1, 3, 4)))
-        blocks.append(jnp.stack(members, axis=3))
-    return jnp.stack(blocks, axis=2).reshape(tiles_x, tiles_y, 64, KZ)
-
-
 def local(cell_offsets, cell_z, frac, charges, tile_counts):
     block_x = KX // lax.axis_size("grp")
     block_y = KY // lax.axis_size("pen")
-    tiles_x = block_x // 2
-    tiles_y = block_y // 2
-    slots = charges.shape[0] // (tiles_x * tiles_y)
-    offsets = cell_offsets.reshape(2, tiles_x, tiles_y, slots)
-    zcell = cell_z.reshape(tiles_x, tiles_y, slots)
-    fracs = frac.reshape(3, tiles_x, tiles_y, slots)
-    charge = charges.reshape(tiles_x, tiles_y, slots)
-    counts = tile_counts.reshape(tiles_x, tiles_y)
-    weight_x, grade_x, weight_y, grade_y, weight_z, grade_z, live_q = tile_weights(
-        offsets, zcell, fracs, charge, counts, KZ
-    )
-    pair = weight_x[..., :, None, :] * weight_y[..., None, :, :] * live_q[..., None, None, :]
-    pair = pair.reshape(tiles_x, tiles_y, 64, slots)
-    spread = jnp.einsum("abfs,absz->abfz", pair, weight_z, precision=highest)
-    padded = place_tiles(spread, tiles_x, tiles_y)
+    tiles = tile_counts.shape[0]
+    slots = charges.shape[0] // tiles
+    width = 4 * slots
+    groups = tiles // 4
+    per_row = block_y // 8
+    live = jnp.arange(slots, dtype=jnp.int32)[None, :] < tile_counts[:, None]
+    live_q = (charges.reshape(tiles, slots) * live.astype(jnp.float32)).reshape(groups, width)
+    offsets = cell_offsets.reshape(2, groups, width)
+    zcell = cell_z.reshape(groups, width)
+    fracs = frac.reshape(3, groups, width)
+    vmem = pl.BlockSpec(memory_space=pltpu.VMEM)
+    params = pltpu.CompilerParams(vmem_limit_bytes=60 * 1024 * 1024)
+    padded = pl.pallas_call(
+        functools.partial(spread_kernel, per_row, slots),
+        out_shape=jax.ShapeDtypeStruct((block_x + 8, block_y + 8, KZ), jnp.float32),
+        in_specs=[vmem] * 4,
+        out_specs=vmem,
+        compiler_params=params,
+        name="spread",
+    )(offsets, zcell, fracs, live_q)
     rim_y = shifted(padded[: block_x + 5, block_y : block_y + 5], "pen", 1)
     merged = padded[: block_x + 5, :block_y].at[:, :5].add(rim_y)
     rim_x = shifted(merged[block_x : block_x + 5], "grp", 1)
     grid = merged[:block_x].at[:5].add(rim_x)
     potential, spectral = spectrum_pen_first(grid, block_x, block_y)
     upper = shifted(potential[:5], "grp", -1)
-    ext_x = jnp.concatenate([potential, upper, jnp.zeros((1, block_y, KZ), jnp.float32)], axis=0)
-    beside = shifted(ext_x[:, :5], "pen", -1)
-    extended = jnp.concatenate(
-        [ext_x, beside, jnp.zeros((block_x + 6, 1, KZ), jnp.float32)], axis=1
-    )
-    footing = gather_tiles(extended, tiles_x, tiles_y)
-    main = jnp.einsum("abfz,absz->abfs", footing, weight_z, precision=highest).reshape(
-        tiles_x, tiles_y, 8, 8, slots
-    )
-    tilt = jnp.einsum("abfz,absz->abfs", footing, grade_z, precision=highest).reshape(
-        tiles_x, tiles_y, 8, 8, slots
-    )
-    force_x = -live_q * jnp.einsum(
-        "abxs,abys,abxys->abs", grade_x, weight_y, main, precision=highest
-    )
-    force_y = -live_q * jnp.einsum(
-        "abxs,abys,abxys->abs", weight_x, grade_y, main, precision=highest
-    )
-    force_z = -live_q * jnp.einsum(
-        "abxs,abys,abxys->abs", weight_x, weight_y, tilt, precision=highest
-    )
+    ext_x = jnp.concatenate([potential[:, :5], upper[:, :5]], axis=0)
+    beside = shifted(ext_x, "pen", -1)
+    beside = jnp.pad(beside, ((0, 0), (0, 3), (0, 0)))
+    forces = pl.pallas_call(
+        functools.partial(interp_kernel, per_row, slots),
+        out_shape=jax.ShapeDtypeStruct((3, groups, width), jnp.float32),
+        in_specs=[vmem] * 7,
+        out_specs=vmem,
+        scratch_shapes=[pltpu.VMEM((block_x + 8, block_y + 8, KZ), jnp.float32)],
+        compiler_params=params,
+        name="interp",
+    )(offsets, zcell, fracs, live_q, potential, upper, beside)
     total = lax.psum(spectral, ("grp", "pen"))
-    forces = jnp.stack([force_x, force_y, force_z], axis=0).reshape(3, tiles_x * tiles_y * slots)
-    return (forces, total / ATOMS)
+    return (forces.reshape(3, groups * width), total / ATOMS)
 
 
 def solution(mesh):

time: 1150 us -> 484 us (0.42)
  local copies, waits for them, and re-layouts: 446 us -> 120 us
  matrix products: 265 us -> 31.1 us
  other arithmetic: 201 us -> 10.7 us
  Pallas kernels: 0 us -> 83.8 us
    dot_general x3 -> x0, matrix products: 225 us -> none  [the longest x1 141 us: local(): spread = jnp.einsum('abfs,absz->abfz', pair, weight_z, precision=highest)]
    reshape x35 -> x2, local copies, waits for them, and re-layouts: 189 us -> 2.54 us  [the longest x1 1.59 us: local(): zcell = cell_z.reshape(groups, width)]
    dot_general x4 -> x0, other arithmetic: 118 us -> none  [the longest x2 60.3 us: local(): jnp.einsum('abxs,abys,abxys->abs', grade_x, weight_y, main, precision=hig...]
    transpose x17 -> x0, local copies, waits for them, and re-layouts: 86.3 us -> none  [place_tiles(): jnp.transpose(shaped[:, :, i, :, j], (0, 2, 1, 3, 4))]
    pallas_call x0 -> x2, Pallas kernels: none -> 83.8 us  [the longest x1 50.6 us: local(): pl.pallas_call(functools.partial(interp_kernel, per_row, slots), out_shap...]
    another operation x5 -> x0, local copies, waits for them, and re-layouts: 46.7 us -> none  [the longest x1 46.1 us: gather_tiles(): return jnp.stack(blocks, axis=2).reshape(tiles_x, tiles_y, 64, KZ)]
    another operation x6 -> x0, other arithmetic: 41.4 us -> none  [the longest x5 40.2 us: gather_tiles(): return jnp.stack(blocks, axis=2).reshape(tiles_x, tiles_y, 64, KZ)]
    add x5 -> x1, other arithmetic: 19 us -> 1.26 us  [local(): merged = padded[:block_x + 5, :block_y].at[:, :5].add(rim_y)]
  transfers between devices with their start and end apart: 5 -> 5, of which waited for: 3 -> 4; matrix products, arithmetic and copies ran while one was open for 12% -> 1% of each run, Pallas kernels for 0% -> 0%
where the time goes in v1:
time: 484 us; the launch traced here: 479 us
  blocking collectives  156 us (32%)
  local copies, waits for them, and re-layouts  120 us (25%)
  Pallas kernels  83.8 us (17%)
  waiting for transfers between devices  65.4 us (14%)
  matrix products  31.1 us (6%)
  other arithmetic  10.7 us (2%)
  starting transfers between devices  8.78 us (2%)
    all_to_all x1, blocking collectives, spectrum_pen_first(): lax.all_to_all(returning, 'grp', split_axis=0, concat_axis=1, tiled=True)  54 us
    pallas_call x1, Pallas kernels, local(): pl.pallas_call(functools.partial(interp_kernel, per_row, slots), out_shap...  50.6 us
    all_to_all x1, waiting for transfers between devices, spectrum_pen_first(): lax.all_to_all(sectioned, 'grp', split_axis=1, concat_axis=0, tiled=True)  50.4 us
    psum x1, blocking collectives, local(): total = lax.psum(spectral, ('grp', 'pen'))  39.6 us
    pallas_call x1, Pallas kernels, local(): pl.pallas_call(functools.partial(spread_kernel, per_row, slots), out_shap...  33.2 us
    all_to_all x1, blocking collectives, spectrum_pen_first(): lax.all_to_all(outgoing, 'pen', split_axis=1, concat_axis=0, tiled=True)  31.4 us
    all_to_all x1, blocking collectives, spectrum_pen_first(): lax.all_to_all(leaving, 'pen', split_axis=0, concat_axis=1, tiled=True)  30.7 us
    unnamed x11, local copies, waits for them, and re-layouts  16 us
  transfers between devices with their start and end apart: 5, of which 4 were waited for; matrix products, arithmetic and copies ran while one was open for 1% of the time, Pallas kernels for 0%

profile of v1, /device:TPU:0, one launch (start us, length us, event | category | flops | bytes accessed | tf_op | source)
XLA Modules:
  0.0 479.2 jit_solution(18155360834866523909)
XLA Ops:
  8.5 33.2 %spread.1 = f32[72,40,256]{2,1,0:T(8,128)} custom-call(s32[2,128,256]{2,1,0:T(8,128)} %bitcast.228, s32[128,256]{1,0:T(8,128)} %reshape.740.z_ref, f32[3,128,256]{2,1,0:T(8,128)} %bitcast.226, f32[128,256]{1,0:T(8,128)} %compare_select_fusion.q_ref), custom_call_target="tpu_custom_call" | custom-call | tf_op jit(solution)/shard_map/spread/pallas_call | solution.py:316
  45.8 5.7 %collective-permute-done = f32[69,5,256]{2,0,1:T(8,128)S(1)} collective-permute-done((f32[69,5,256]{2,0,1:T(8,128)S(1)}, f32[69,5,256]{2,0,1:T(8,128)S(1)}, u32[]{:S(2)}, u32[]{:S(2)}) %collective-permute-start) | collective-permute-done | bytes 353312 | tf_op jit(solution)/shard_map/ppermute | solution.py:24
  52.7 5.7 %scatter-add.6 = f32[69,32,256]{2,1,0:T(8,128)S(1)} dynamic-update-slice(f32[69,32,256]{2,1,0:T(8,128)S(1)} %slice.164, f32[69,5,256]{2,1,0:T(8,128)S(1)} %slice_add_fusion, s32[]{:T(128)} %constant.318.clone.1, s32[]{:T(128)} %constant.318.clone.1, s32[]{:T(128)} %constant.318.clone.1) | dynamic-update-slice | bytes 706564 | tf_op jit(solution)/shard_map/scatter-add | solution.py:325
  58.4 2.6 collective-permute-start.1
  61.2 5.2 %collective-permute-done.1 = f32[5,32,256]{2,1,0:T(8,128)S(1)} collective-permute-done((f32[5,32,256]{2,1,0:T(8,128)S(1)}, f32[5,32,256]{2,1,0:T(8,128)S(1)}, u32[]{:S(2)}, u32[]{:S(2)}) %collective-permute-start.1) | collective-permute-done | bytes 163872 | tf_op jit(solution)/shard_map/ppermute | solution.py:24
  66.4 2.6 negate_bitcast_fusion
  69.0 2.6 fusion.19
  71.6 2.3 pad_maximum_fusion
  73.9 7.5 %copy.101 = f32[32,136,2,64]{3,2,1,0:T(2,128)} copy(f32[32,136,2,64]{1,3,0,2:T(8,128)} %pad_maximum_fusion) | data formatting | bytes 4456448 | tf_op jit(solution)/shard_map/stack | solution.py:265
  81.4 4.6 all_to_all.52
  86.5 31.4 %all_to_all.70 = f32[32,8,2176]{2,0,1:T(8,128)} all-to-all(f32[32,8,2176]{2,0,1:T(8,128)S(1)} %copy.102), channel_id=1, replica_groups=mesh['grp'=4,'pen'=8] {'pen'}, dimensions={1} | all-to-all | bytes 4456448 | tf_op jit(solution)/shard_map/all_to_all | solution.py:266
  117.9 2.0 copy.103
  119.9 2.1 fusion.8
  122.0 2.1 fusion.54
  124.6 5.1 %copy.107 = f32[64,256,17,2]{0,3,2,1:T(2,128)} copy(f32[64,256,17,2]{1,0,2,3:T(8,128)S(1)} %maximum_bitcast_fusion) | data formatting | bytes 4456448 | tf_op jit(solution)/shard_map/transpose | solution.py:268
  129.7 5.2 %copy.108 = f32[64,4,2176]{2,0,1:T(8,128)} copy(f32[64,4,2176]{0,2,1:T(8,128)} %bitcast.216) | data formatting | bytes 4456448 | tf_op jit(solution)/shard_map/all_to_all | solution.py:271
  134.9 4.1 all-to-all-start.1
  139.5 50.4 %all-to-all-done.1 = f32[64,4,2176]{2,0,1:T(8,128)S(1)} async-done(((f32[64,4,2176]{2,0,1:T(8,128)}), f32[64,4,2176]{2,0,1:T(8,128)S(1)}, u32[]{:S(2)}, u32[]{:S(2)}) %all-to-all-start.1) | async-done | bytes 2228256 | tf_op jit(solution)/shard_map/all_to_all | solution.py:271
  189.9 1.9 copy.109
  191.9 2.9 dot_general.59
  194.7 2.1 fusion.6
  196.8 2.0 fusion.12
  202.4 2.6 reshape.743
  205.0 3.0 dot_general.63
  208.1 2.1 fusion.4
  210.1 2.0 fusion.10
  214.5 4.8 %all_to_all.60 = f32[4,64,2176]{1,0,2:T(4,128)} reshape(f32[256,64,17,2]{0,3,2,1:T(2,128)S(1)} %copy.121) | data formatting | bytes 4456448 | tf_op jit(solution)/shard_map/all_to_all | solution.py:283
  219.3 4.5 copy.122
  223.8 54.0 %all_to_all.71 = f32[4,64,2176]{2,1,0:T(8,128)} all-to-all(f32[4,64,2176]{2,1,0:T(8,128)S(1)} %copy.122), channel_id=1, replica_groups=mesh['grp'=4,'pen'=8] {'grp'}, dimensions={0} | all-to-all | bytes 4456448 | tf_op jit(solution)/shard_map/all_to_all | solution.py:283
  277.9 4.7 copy.123
  282.6 5.9 %copy.147 = f32[256,17,2,64]{0,3,1,2:T(8,128)S(1)} copy(f32[256,17,2,64]{3,2,1,0:T(2,128)} %bitcast.212) | data formatting | bytes 4456448 | tf_op jit(solution)/shard_map/dot_general | solution.py:250
  288.5 7.0 %copy.124 = f32[256,17,2,64]{0,3,2,1:T(8,128)} copy(f32[256,17,2,64]{3,2,1,0:T(2,128)} %bitcast.213) | data formatting | bytes 4456448 | tf_op jit(solution)/shard_map/transpose | solution.py:284
  295.5 3.7 fusion.2
  299.2 2.1 fusion
  301.8 5.1 %copy.128 = f32[256,17,2,64]{3,2,1,0:T(2,128)} copy(f32[256,17,2,64]{0,3,1,2:T(8,128)S(1)} %pad_maximum_fusion.3) | data formatting | bytes 4456448 | tf_op jit(solution)/shard_map/stack | solution.py:288
  306.9 4.6 all_to_all.63
  311.6 30.7 %all_to_all.72 = f32[8,32,2176]{2,1,0:T(8,128)S(1)} all-to-all(f32[8,32,2176]{2,1,0:T(8,128)S(1)} %all_to_all.63), channel_id=1, replica_groups=mesh['grp'=4,'pen'=8] {'pen'}, dimensions={0} | all-to-all | bytes 4456448 | tf_op jit(solution)/shard_map/all_to_all | solution.py:289
  343.5 4.1 reshape.746
  347.6 8.8 %fusion.189 = (f32[32,136,1,64]{3,2,1,0:T(1,128)}, f32[32,136,1,64]{3,2,1,0:T(1,128)S(1)}) fusion(f32[32,136,2,64]{3,2,1,0:T(2,128)} %reshape.746), kind=kLoop, calls=%fused_computation.269 | loop fusion | bytes 4456448 | tf_op jit(solution)/shard_map/slice | solution.py:293
  356.4 5.8 %copy.152 = f32[32,136,1,64]{1,3,0,2:T(8,128)} copy(f32[32,136,1,64]{3,2,1,0:T(1,128)} %get-tuple-element.80) | data formatting | bytes 2228224
  362.2 4.5 fusion.67
  366.7 4.5 copy.153
  371.3 3.4 fusion.65
  374.7 2.3 fusion.14.pot_ref
  378.5 4.2 collective-permute-done.2.up_ref
  383.6 39.6 %psum.7 = f32[]{:T(128)} all-reduce(f32[]{:T(128)S(6)} %mul_shard_map.3), channel_id=1, replica_groups=mesh['grp'=4,'pen'=8] {'grp','pen'}, use_global_device_ids=true, to_apply=%region_1.6 | all-reduce | flops 1 | bytes 8 | tf_op jit(solution)/shard_map/psum | solution.py:342
  424.9 50.6 %interp.1 = f32[3,128,256]{2,1,0:T(8,128)} custom-call(s32[2,128,256]{2,1,0:T(8,128)} %bitcast.229, s32[128,256]{1,0:T(8,128)} %reshape.740.z_ref, f32[3,128,256]{2,1,0:T(8,128)} %bitcast.227, f32[128,256]{1,0:T(8,128)} %compare_select_fusion.q_ref, f32[64,32,256]{2,1,0:T(8,128)} %copy-done, f32[5,32,256]{2,1,0:T(8,128)} %copy-done.2, f32[69,8,256]{2,1,0:T(8,128)} %pad.8.side_ref), custom_call_target="tpu_custom_call" | custom-call | tf_op jit(solution)/shard_map/interp/pallas_call | solution.py:333
  475.5 2.1 copy.156
  (67 shorter events, 25.3 us)
Async XLA Ops:
  42.9 8.6 %collective-permute-start = (f32[69,5,256]{2,0,1:T(8,128)S(1)}, f32[69,5,256]{2,0,1:T(8,128)S(1)}, u32[]{:S(2)}, u32[]{:S(2)}) collective-permute-start(f32[69,5,256]{2,0,1:T(8,128)S(1)} %copy.97), channel_id=1, source_target_pairs={{7,0},{0,1},{1,2},{2,3},{3,4},{4,5},{5,6},{6,7},{15,8},{8,9},{9,10... | collective-permute-start | bytes 1059848 | tf_op jit(solution)/shard_map/ppermute | solution.py:24
  58.4 7.9 %collective-permute-start.1 = (f32[5,32,256]{2,1,0:T(8,128)S(1)}, f32[5,32,256]{2,1,0:T(8,128)S(1)}, u32[]{:S(2)}, u32[]{:S(2)}) collective-permute-start(f32[5,32,256]{2,1,0:T(8,128)S(1)} %slice.169), channel_id=1, source_target_pairs={{24,0},{0,8},{8,16},{16,24},{25,1},{1,9},{9,17},{17,25},{26,2},{2,... | collective-permute-start | bytes 491528 | tf_op jit(solution)/shard_map/ppermute | solution.py:24
  134.9 55.1 %all-to-all-start.1 = ((f32[64,4,2176]{2,0,1:T(8,128)}), f32[64,4,2176]{2,0,1:T(8,128)S(1)}, u32[]{:S(2)}, u32[]{:S(2)}) async-start(f32[64,4,2176]{2,0,1:T(8,128)} %copy.108), calls=%async_computation.1 | async-start | bytes 4456448 | tf_op jit(solution)/shard_map/all_to_all | solution.py:271
  371.3 3.4 copy-start.1
  377.0 47.0 %copy-start = (f32[64,32,256]{2,1,0:T(8,128)}, f32[64,32,256]{2,1,0:T(8,128)S(1)}, u32[]{:S(2)}) copy-start(f32[64,32,256]{2,1,0:T(8,128)S(1)} %fusion.14.pot_ref) | copy-start | bytes 6291460
  377.0 5.7 %collective-permute-start.2 = (f32[5,32,256]{2,1,0:T(8,128)S(1)}, f32[5,32,256]{2,1,0:T(8,128)S(1)}, u32[]{:S(2)}, u32[]{:S(2)}) collective-permute-start(f32[5,32,256]{2,1,0:T(8,128)S(1)} %slice.188), channel_id=1, source_target_pairs={{8,0},{16,8},{24,16},{0,24},{9,1},{17,9},{25,17},{1,25},{10,2},{18... | collective-permute-start | bytes 491528 | tf_op jit(solution)/shard_map/ppermute | solution.py:24
  382.7 42.1 %copy-start.2 = (f32[5,32,256]{2,1,0:T(8,128)}, f32[5,32,256]{2,1,0:T(8,128)S(1)}, u32[]{:S(2)}) copy-start(f32[5,32,256]{2,1,0:T(8,128)S(1)} %collective-permute-done.2.up_ref) | copy-start | bytes 491524
  382.9 40.9 %collective-permute-start.3 = (f32[69,5,256]{2,0,1:T(8,128)S(1)}, f32[69,5,256]{2,0,1:T(8,128)S(1)}, u32[]{:S(2)}, u32[]{:S(2)}) collective-permute-start(f32[69,5,256]{2,0,1:T(8,128)S(1)} %copy.134), channel_id=1, source_target_pairs={{1,0},{2,1},{3,2},{4,3},{5,4},{6,5},{7,6},{0,7},{9,8},{10,9},{11,1... | collective-permute-start | bytes 1059848 | tf_op jit(solution)/shard_map/ppermute | solution.py:24

commit v2 on v1

--- a/solution.py
+++ b/solution.py
@@ -3,6 +3,7 @@
 
 import jax
 import jax.numpy as jnp
+import numpy as np
 from jax import lax
 from jax.experimental import pallas as pl
 from jax.experimental.pallas import tpu as pltpu
@@ -213,89 +214,182 @@
     return jnp.where(square > 0, value, 0.0)
 
 
-def dft_tables(length):
-    index = jnp.arange(length, dtype=jnp.int32)
-    angle = (index[:, None] * index[None, :] % length).astype(jnp.float32) * (
-        2.0 * math.pi / length
-    )
-    return (jnp.cos(angle), jnp.sin(angle))
-
-
-def z_slots(groups):
-    planes = KZ // (2 * groups) + 1
-    owner = jnp.arange(groups, dtype=jnp.int32)[:, None]
-    within = jnp.arange(planes, dtype=jnp.int32)[None, :]
-    ordinary = owner * (planes - 1) + within
-    frequency = jnp.where(within < planes - 1, ordinary, jnp.where(owner == 0, KZ // 2, 0))
+def waves(index, length):
+    angle = (index % length) * (2.0 * math.pi / length)
+    return (np.cos(angle), np.sin(angle))
+
+
+def z_table(groups):
+    planes = KZ // (2 * groups)
+    frequency = np.arange(KZ // 2).reshape(groups, planes)
+    cos, sin = waves(frequency[..., None] * np.arange(KZ), KZ)
+    table = np.stack([cos, -sin], axis=1)
+    table[0, 1, 0] = waves(np.arange(KZ) * (KZ // 2), KZ)[0]
+    weight = np.full((groups, 2, planes), 2.0)
+    weight[0, :, 0] = 1.0
+    table = table.reshape(KZ, KZ)
+    return (table.astype(np.float32), (table * weight.reshape(KZ, 1)).astype(np.float32))
+
+
+def block_table(frequency, length, groups):
+    position = np.arange(length)
+    cos, sin = waves(frequency[..., None] * position, length)
+    shape = (frequency.shape[0], frequency.shape[1], groups, length // groups)
+    cos, sin = cos.reshape(shape), sin.reshape(shape)
+    real_row = np.stack([cos, sin], axis=3)
+    imag_row = np.stack([-sin, cos], axis=3)
+    table = np.stack([real_row, imag_row], axis=1)
+    return table.reshape(2 * length, 2 * length).astype(np.float32)
+
+
+def y_frequency(groups):
+    first = np.arange(KY // 2).reshape(groups, -1)
+    second = np.where(first == 0, KY // 2, (KY - first) % KY)
+    return np.concatenate([first, second], axis=1)
+
+
+def exchange_kernel(axis, count, *refs):
+    arrays = (len(refs) - 3) // 2
+    sources, targets = refs[:arrays], refs[arrays : 2 * arrays]
+    send_sem, recv_sem, own_sem = refs[2 * arrays :]
+    me = lax.axis_index(axis)
+    barrier = pltpu.get_barrier_semaphore()
+    for d in range(1, count):
+        pl.semaphore_signal(
+            barrier,
+            inc=1,
+            device_id={axis: lax.rem(me + d, count)},
+            device_id_type=pl.DeviceIdType.MESH,
+        )
+    pl.semaphore_wait(barrier, count - 1)
+    copies = []
+    for k in range(arrays):
+        for d in range(1, count):
+            peer = lax.rem(me + d, count)
+            copies.append(
+                pltpu.make_async_remote_copy(
+                    src_ref=sources[k].at[peer],
+                    dst_ref=targets[k].at[me],
+                    send_sem=send_sem.at[k, d],
+                    recv_sem=recv_sem.at[k, d],
+                    device_id={axis: peer},
+                    device_id_type=pl.DeviceIdType.MESH,
+                )
+            )
+        copies.append(
+            pltpu.make_async_copy(sources[k].at[me], targets[k].at[me], own_sem.at[k])
+        )
+    for copy in copies:
+        copy.start()
+    for copy in copies:
+        copy.wait()
+
+
+def exchange(arrays, axis, number):
+    count = lax.axis_size(axis)
+    vmem = pl.BlockSpec(memory_space=pltpu.VMEM)
+    return pl.pallas_call(
+        functools.partial(exchange_kernel, axis, count),
+        out_shape=[jax.ShapeDtypeStruct(array.shape, array.dtype) for array in arrays],
+        in_specs=[vmem] * len(arrays),
+        out_specs=[vmem] * len(arrays),
+        scratch_shapes=[
+            pltpu.SemaphoreType.DMA((len(arrays), count)),
+            pltpu.SemaphoreType.DMA((len(arrays), count)),
+            pltpu.SemaphoreType.DMA((len(arrays),)),
+        ],
+        compiler_params=pltpu.CompilerParams(collective_id=number, has_side_effects=True),
+        name="exchange" + str(number),
+    )(*arrays)
+
+
+def dot(left, right, left_dim, right_dim):
+    dims = (((left_dim,), (right_dim,)), ((), ()))
+    return lax.dot_general(
+        left, right, dims, precision=highest, preferred_element_type=jnp.float32
+    )
+
+
+def spectrum_of(grid, block_x, block_y):
+    grp, pen = lax.axis_size("grp"), lax.axis_size("pen")
+    planes = KZ // (2 * pen)
+    lines = KY // grp
+    half = lines // 2
+    forward_z, backward_z = z_table(pen)
+    order_y = y_frequency(grp)
+    table_y = block_table(order_y, KY, pen)
+    table_x = block_table(np.arange(KX)[None], KX, grp)
+    lines_z = dot(forward_z, grid.reshape(block_x * block_y, KZ), 1, 1)
+    lines_z = lines_z.reshape(pen, 2, planes, block_x, block_y).transpose(0, 1, 4, 2, 3)
+    (columns,) = exchange(
+        [lines_z.reshape(pen, 2 * block_y, planes * block_x)], "pen", 1
+    )
+    lines_y = dot(table_y, columns.reshape(2 * KY, planes * block_x), 1, 0)
+    lines_y = lines_y.reshape(grp, 2, lines, planes, block_x).transpose(0, 1, 4, 3, 2)
+    (rows,) = exchange([lines_y.reshape(grp, 2 * block_x, planes * lines)], "grp", 2)
+    rows = rows.reshape(grp, 2, block_x, planes * lines)
+    at_grp, at_pen = lax.axis_index("grp"), lax.axis_index("pen")
+    packed = rows[..., :lines]
+    alone = (at_grp == 0) & (jnp.arange(lines) % half == 0)
+    partner = jnp.where(
+        alone, packed, jnp.concatenate([packed[..., half:], packed[..., :half]], axis=-1)
+    )
+    a, b = packed[:, :1], packed[:, 1:]
+    c, d = partner[:, :1], partner[:, 1:]
+    whole = jnp.concatenate([a + c, b - d], axis=1) * 0.5
+    midway = jnp.concatenate([b + d, c - a], axis=1) * 0.5
+    origin = at_pen == 0
+    whole = jnp.where(origin, whole, packed)
+    midway = jnp.where(origin, midway, 0.0)
+    total_lanes = (planes + 1) * lines
+    full = jnp.concatenate([whole, rows[..., lines:], midway], axis=-1)
+    spectrum = dot(table_x, full.reshape(2 * KX, total_lanes), 1, 0)
+    spectrum = spectrum.reshape(2, KX, total_lanes)
+    index_x = jnp.arange(KX, dtype=jnp.int32)[:, None]
+    slot = jnp.arange(planes + 1, dtype=jnp.int32)
+    index_z = jnp.where(slot < planes, at_pen * planes + slot, KZ // 2)
     plane_weight = jnp.where(
-        within < planes - 1, jnp.where(frequency == 0, 1.0, 2.0), jnp.where(owner == 0, 1.0, 0.0)
-    )
-    frequency = frequency.reshape(-1)
-    plane_weight = plane_weight.reshape(-1).astype(jnp.float32)
-    position = jnp.arange(KZ, dtype=jnp.int32)
-    angle = (frequency[:, None] * position[None, :] % KZ).astype(jnp.float32) * (2.0 * math.pi / KZ)
-    usable = (plane_weight > 0).astype(jnp.float32)[:, None]
-    return (planes, frequency, plane_weight, jnp.cos(angle) * usable, jnp.sin(angle) * usable)
-
-
-def forward_complex(data, cos_table, sin_table, shape, axis):
-    direct = jnp.dot(cos_table, data, precision=highest).reshape(shape)
-    other = jnp.dot(sin_table, data, precision=highest).reshape(shape)
-    real_part = jnp.take(direct, 0, axis=axis) + jnp.take(other, 1, axis=axis)
-    imag_part = jnp.take(direct, 1, axis=axis) - jnp.take(other, 0, axis=axis)
-    return (real_part, imag_part)
-
-
-def inverse_complex(data, cos_table, sin_table, shape, axis):
-    direct = jnp.dot(cos_table, data, precision=highest).reshape(shape)
-    other = jnp.dot(sin_table, data, precision=highest).reshape(shape)
-    real_part = jnp.take(direct, 0, axis=axis) - jnp.take(other, 1, axis=axis)
-    imag_part = jnp.take(other, 0, axis=axis) + jnp.take(direct, 1, axis=axis)
-    return (real_part, imag_part)
-
-
-def spectrum_pen_first(grid, block_x, block_y):
-    cos_x, sin_x = dft_tables(KX)
-    cos_y, sin_y = dft_tables(KY)
-    planes, frequency, plane_weight, cos_z, sin_z = z_slots(lax.axis_size("pen"))
-    slot_total = cos_z.shape[0]
-    lines = KY // lax.axis_size("grp")
-    real_z = jnp.einsum("xyz,kz->ykx", grid, cos_z, precision=highest)
-    imag_z = -jnp.einsum("xyz,kz->ykx", grid, sin_z, precision=highest)
-    outgoing = jnp.stack([real_z, imag_z], axis=2).reshape(block_y, slot_total * 2 * block_x)
-    columns = lax.all_to_all(outgoing, "pen", split_axis=1, concat_axis=0, tiled=True)
-    real_y, imag_y = forward_complex(columns, cos_y, sin_y, (KY, planes, 2, block_x), 2)
-    sectioned = jnp.transpose(jnp.stack([real_y, imag_y], axis=-1), (2, 0, 1, 3)).reshape(
-        block_x, KY * planes * 2
-    )
-    rows = lax.all_to_all(sectioned, "grp", split_axis=1, concat_axis=0, tiled=True)
-    real_x, imag_x = forward_complex(rows, cos_x, sin_x, (KX, lines, planes, 2), 3)
-    first = lax.axis_index("pen") * planes
-    index_x = jnp.arange(KX, dtype=jnp.int32)[:, None, None]
-    index_y = lax.axis_index("grp") * lines + jnp.arange(lines, dtype=jnp.int32)[None, :, None]
-    index_z = lax.dynamic_slice_in_dim(frequency, first, planes)[None, None, :]
-    local_weight = lax.dynamic_slice_in_dim(plane_weight, first, planes)[None, None, :]
+        slot < planes,
+        jnp.where(origin & (slot == 0), 1.0, 2.0),
+        jnp.where(origin, 1.0, 0.0),
+    )
+    index_z = jnp.repeat(index_z, lines)[None, :]
+    plane_weight = jnp.repeat(plane_weight, lines)[None, :]
+    index_y = lax.dynamic_index_in_dim(jnp.asarray(order_y, jnp.int32), at_grp, 0, False)
+    index_y = jnp.tile(index_y, planes + 1)[None, :]
     kernel = influence(index_x, index_y, index_z)
-    spectral = 0.5 * jnp.sum(local_weight * kernel * (real_x * real_x + imag_x * imag_x))
-    scaled = jnp.stack([kernel * real_x, kernel * imag_x], axis=-1).reshape(KX, lines * planes * 2)
-    real_b, imag_b = inverse_complex(scaled, cos_x, sin_x, (KX, lines, planes, 2), 3)
-    returning = jnp.stack([real_b, imag_b], axis=-1).reshape(KX, lines * planes * 2)
-    rows_home = lax.all_to_all(returning, "grp", split_axis=0, concat_axis=1, tiled=True)
-    rows_home = jnp.transpose(rows_home.reshape(block_x, KY, planes, 2), (1, 2, 3, 0)).reshape(
-        KY, planes * 2 * block_x
-    )
-    real_c, imag_c = inverse_complex(rows_home, cos_y, sin_y, (KY, planes, 2, block_x), 2)
-    leaving = jnp.stack([real_c, imag_c], axis=2).reshape(KY, planes * 2 * block_x)
-    home = lax.all_to_all(leaving, "pen", split_axis=0, concat_axis=1, tiled=True).reshape(
-        block_y, slot_total, 2, block_x
-    )
-    potential = jnp.einsum(
-        "ykx,kz->xyz", home[:, :, 0], plane_weight[:, None] * cos_z, precision=highest
-    )
-    potential = potential - jnp.einsum(
-        "ykx,kz->xyz", home[:, :, 1], plane_weight[:, None] * sin_z, precision=highest
-    )
-    return (potential, spectral)
+    power = spectrum[0] * spectrum[0] + spectrum[1] * spectrum[1]
+    spectral = 0.5 * jnp.sum(plane_weight * kernel * power)
+    scaled = (spectrum * kernel).reshape(2 * KX, total_lanes)
+    returning = dot(table_x, scaled, 0, 0).reshape(grp, 2, block_x, total_lanes)
+    midway = returning[..., planes * lines :]
+    turned = jnp.concatenate([-midway[:, 1:], midway[:, :1]], axis=1)
+    returning = jnp.concatenate(
+        [returning[..., :lines] + turned, returning[..., lines : planes * lines]], axis=-1
+    )
+    rows, sums = exchange(
+        [
+            returning.reshape(grp, 2 * block_x, planes * lines),
+            jnp.broadcast_to(spectral, (grp, 8, 128)),
+        ],
+        "grp",
+        3,
+    )
+    spectral = jnp.sum(sums[:, 0, 0])
+    rows = rows.reshape(grp, 2, block_x, planes, lines).transpose(0, 1, 4, 3, 2)
+    columns = dot(table_y, rows.reshape(2 * KY, planes * block_x), 0, 0)
+    columns, sums = exchange(
+        [
+            columns.reshape(pen, 2 * block_y, planes * block_x),
+            jnp.broadcast_to(spectral, (pen, 8, 128)),
+        ],
+        "pen",
+        4,
+    )
+    spectral = jnp.sum(sums[:, 0, 0])
+    home = columns.reshape(pen, 2, block_y, planes, block_x).transpose(0, 1, 3, 4, 2)
+    potential = dot(home.reshape(KZ, block_x * block_y), backward_z, 0, 0)
+    return (potential.reshape(block_x, block_y, KZ), spectral)
 
 
 def local(cell_offsets, cell_z, frac, charges, tile_counts):
@@ -325,7 +419,7 @@
     merged = padded[: block_x + 5, :block_y].at[:, :5].add(rim_y)
     rim_x = shifted(merged[block_x : block_x + 5], "grp", 1)
     grid = merged[:block_x].at[:5].add(rim_x)
-    potential, spectral = spectrum_pen_first(grid, block_x, block_y)
+    potential, total = spectrum_of(grid, block_x, block_y)
     upper = shifted(potential[:5], "grp", -1)
     ext_x = jnp.concatenate([potential[:, :5], upper[:, :5]], axis=0)
     beside = shifted(ext_x, "pen", -1)
@@ -339,7 +433,6 @@
         compiler_params=params,
         name="interp",
     )(offsets, zcell, fracs, live_q, potential, upper, beside)
-    total = lax.psum(spectral, ("grp", "pen"))
     return (forces.reshape(3, groups * width), total / ATOMS)
 
 

time: 484 us -> 400 us (0.83)
  Pallas kernels: 83.8 us -> 245 us
  blocking collectives: 156 us -> 0 us
  waiting for transfers between devices: 65.4 us -> 16.8 us
  local copies, waits for them, and re-layouts: 120 us -> 94.5 us
  matrix products: 31.1 us -> 18.9 us
    pallas_call x0 -> x4, Pallas kernels: none -> 161 us  [exchange(): pl.pallas_call(functools.partial(exchange_kernel, axis, count), out_shape...]
    all_to_all x3 -> x0, blocking collectives: 116 us -> none  [the longest x1 54 us: spectrum_pen_first(): lax.all_to_all(returning, 'grp', split_axis=0, concat_axis=1, tiled=True)]
    all_to_all x1 -> x0, waiting for transfers between devices: 50.4 us -> none  [spectrum_pen_first(): lax.all_to_all(sectioned, 'grp', split_axis=1, concat_axis=0, tiled=True)]
    reshape x2 -> x11, local copies, waits for them, and re-layouts: 6.63 us -> 55.7 us  [the longest x2 11.5 us: spectrum_of(): columns.reshape(pen, 2, block_y, planes, block_x).transpose(0, 1, 3, 4, 2)]
    psum x1 -> x0, blocking collectives: 39.6 us -> none  [local(): total = lax.psum(spectral, ('grp', 'pen'))]
    all_to_all x8 -> x0, local copies, waits for them, and re-layouts: 30.2 us -> none  [the longest x3 14.1 us: spectrum_pen_first(): lax.all_to_all(returning, 'grp', split_axis=0, concat_axis=1, tiled=True)]
    dot_general x5 -> x0, local copies, waits for them, and re-layouts: 15.7 us -> none  [the longest x2 8.95 us: inverse_complex(): direct = jnp.dot(cos_table, data, precision=highest).reshape(shape)]
    another operation x4, local copies, waits for them, and re-layouts: 16.1 us -> 0.83 us  [the longest x3 0.76 us: spectrum_of(): index_y = jnp.tile(index_y, planes + 1)[None, :]]
  transfers between devices with their start and end apart: 5 -> 4, of which waited for: 4 -> 4; matrix products, arithmetic and copies ran while one was open for 1% -> 1% of each run, Pallas kernels for 0% -> 0%
where the time goes in v2:
time: 400 us; the launch traced here: 397 us
  Pallas kernels  245 us (61%)
  local copies, waits for them, and re-layouts  94.5 us (24%)
  matrix products  18.9 us (5%)
  waiting for transfers between devices  16.8 us (4%)
  other arithmetic  12.9 us (3%)
  starting transfers between devices  5.92 us (1%)
    pallas_call x4, Pallas kernels, exchange(): pl.pallas_call(functools.partial(exchange_kernel, axis, count), out_shape...  161 us
    pallas_call x1, Pallas kernels, local(): pl.pallas_call(functools.partial(interp_kernel, per_row, slots), out_shap...  50.6 us
    pallas_call x1, Pallas kernels, local(): pl.pallas_call(functools.partial(spread_kernel, per_row, slots), out_shap...  33.2 us
    dot_general x6, matrix products, dot(): lax.dot_general(left, right, dims, precision=highest, preferred_element_t...  18.9 us
    ppermute x4, waiting for transfers between devices, shifted(): return lax.ppermute(block, axis, route)  16.8 us
    reshape x2, local copies, waits for them, and re-layouts, spectrum_of(): columns.reshape(pen, 2, block_y, planes, block_x).transpose(0, 1, 3, 4, 2)  11.5 us
    reshape x2, local copies, waits for them, and re-layouts, spectrum_of(): rows = rows.reshape(grp, 2, block_x, planes, lines).transpose(0, 1, 4, 3, 2)  10.4 us
    reshape x2, local copies, waits for them, and re-layouts, spectrum_of(): lines_y.reshape(grp, 2, lines, planes, block_x).transpose(0, 1, 4, 3, 2)  8.37 us
  transfers between devices with their start and end apart: 4, of which 4 were waited for; matrix products, arithmetic and copies ran while one was open for 1% of the time, Pallas kernels for 0%

profile of v2, /device:TPU:0, one launch (start us, length us, event | category | flops | bytes accessed | tf_op | source)
XLA Modules:
  0.0 397.4 jit_solution(11274890561456356186)
XLA Ops:
  2.7 1.9 copy.44
  4.6 1.7 copy.45
  7.6 33.2 %spread.1 = f32[72,40,256]{2,1,0:T(8,128)} custom-call(s32[2,128,256]{2,1,0:T(8,128)} %bitcast.72, s32[128,256]{1,0:T(8,128)} %reshape.805.z_ref, f32[3,128,256]{2,1,0:T(8,128)} %bitcast.70, f32[128,256]{1,0:T(8,128)} %compare_select_fusion.2.q_ref), custom_call_target="tpu_custom_call" | custom-call | tf_op jit(solution)/shard_map/spread/pallas_call | solution.py:410
  40.8 1.1 slice.161
  43.2 1.8 slice.159
  45.5 5.0 %collective-permute-done = f32[69,5,256]{2,0,1:T(8,128)S(1)} collective-permute-done((f32[69,5,256]{2,0,1:T(8,128)S(1)}, f32[69,5,256]{2,0,1:T(8,128)S(1)}, u32[]{:S(2)}, u32[]{:S(2)}) %collective-permute-start) | collective-permute-done | bytes 353312 | tf_op jit(solution)/shard_map/ppermute | solution.py:25
  50.6 1.3 slice_add_fusion
  51.9 5.7 %scatter-add.6 = f32[69,32,256]{2,1,0:T(8,128)S(1)} dynamic-update-slice(f32[69,32,256]{2,1,0:T(8,128)S(1)} %slice.159, f32[69,5,256]{2,1,0:T(8,128)S(1)} %slice_add_fusion, s32[]{:T(128)} %constant.246.clone.1, s32[]{:T(128)} %constant.246.clone.1, s32[]{:T(128)} %constant.246.clone.1) | dynamic-update-slice | bytes 706564 | tf_op jit(solution)/shard_map/scatter-add | solution.py:419
  57.6 2.6 collective-permute-start.1
  60.5 4.9 %collective-permute-done.1 = f32[5,32,256]{2,1,0:T(8,128)S(1)} collective-permute-done((f32[5,32,256]{2,1,0:T(8,128)S(1)}, f32[5,32,256]{2,1,0:T(8,128)S(1)}, u32[]{:S(2)}, u32[]{:S(2)}) %collective-permute-start.1) | collective-permute-done | bytes 163872 | tf_op jit(solution)/shard_map/ppermute | solution.py:25
  65.5 1.1 fusion.60
  66.6 4.8 %reshape.809 = f32[8,2,16,64,32]{4,3,2,1,0:T(8,128)} reshape(f32[256,2048]{1,0:T(8,128)S(1)} %fusion.60) | data formatting | bytes 4194304 | tf_op jit(solution)/shard_map/reshape | solution.py:323
  71.4 6.9 %copy.29 = f32[8,2,32,16,64]{4,3,2,1,0:T(8,128)} copy(f32[8,2,32,16,64]{2,4,3,1,0:T(8,128)} %bitcast.49) | data formatting | bytes 4194304 | tf_op jit(solution)/shard_map/transpose | solution.py:323
  78.3 4.8 %reshape.810.refs_0_ = f32[8,64,1024]{2,1,0:T(8,128)} reshape(f32[8,2,32,16,64]{4,3,2,1,0:T(8,128)} %copy.29) | data formatting | bytes 4194304 | tf_op jit(solution)/shard_map/reshape | solution.py:325
  83.1 27.9 %exchange1.1 = f32[8,64,1024]{2,1,0:T(8,128)} custom-call(f32[8,64,1024]{2,1,0:T(8,128)} %reshape.810.refs_0_), custom_call_target="tpu_custom_call" | custom-call | tf_op jit(solution)/shard_map/exchange1/pallas_call | solution.py:291
  111.0 3.4 fusion.61
  114.5 2.5 reshape.812
  117.0 5.8 %copy.30 = f32[4,2,64,16,64]{2,3,4,1,0:T(8,128)} copy(f32[4,2,64,16,64]{4,3,2,1,0:T(8,128)} %reshape.812) | data formatting | bytes 4194304 | tf_op jit(solution)/shard_map/reshape | solution.py:328
  122.9 4.9 %reshape.813.refs_0_ = f32[4,128,1024]{2,1,0:T(8,128)} reshape(f32[4,2,64,16,64]{4,3,2,1,0:T(8,128)} %bitcast.51) | data formatting | bytes 4194304 | tf_op jit(solution)/shard_map/reshape | solution.py:329
  127.7 40.4 %exchange2.1 = f32[4,128,1024]{2,1,0:T(8,128)} custom-call(f32[4,128,1024]{2,1,0:T(8,128)} %reshape.813.refs_0_), custom_call_target="tpu_custom_call" | custom-call | tf_op jit(solution)/shard_map/exchange2/pallas_call | solution.py:291
  168.1 1.2 fusion.59
  169.4 3.5 slice.172
  172.9 1.1 maximum_select_fusion
  174.0 1.0 slice_add_fusion.3
  175.0 1.8 fusion.5
  176.9 3.0 concatenate.28
  179.9 3.4 fusion.62
  183.2 1.9 fusion.4
  187.4 4.3 %fusion = f32[512,1088]{1,0:T(8,128)S(1)} fusion(f32[512,512]{1,0:T(8,128)S(1)} %copy-done.2, f32[512,1088]{0,1:T(8,128)S(1)} %fusion.62, f32[512,1088]{0,1:T(8,128)S(1)} %bitcast.64), kind=kOutput, calls=%fused_computation | convolution fusion | flops 1711833088 | bytes 7733248 | tf_op jit(solution)/shard_map/dot_general | solution.py:308
  192.4 1.9 pad_maximum_fusion
  195.6 63.1 %exchange3.1 = (f32[4,128,1024]{2,1,0:T(8,128)}, f32[4,8,128]{2,1,0:T(8,128)}) custom-call(f32[4,128,1024]{2,1,0:T(8,128)} %bitcast.66, f32[4,8,128]{2,1,0:T(8,128)} %broadcast_in_dim.54.refs_1_), custom_call_target="tpu_custom_call" | custom-call | tf_op jit(solution)/shard_map/exchange3/pallas_call | solution.py:291
  258.7 4.5 %reshape.818 = f32[4,2,64,16,64]{4,3,2,1,0:T(8,128)} reshape(f32[4,128,1024]{2,1,0:T(8,128)} %get-tuple-element.30) | data formatting | bytes 4194304 | tf_op jit(solution)/shard_map/reshape | solution.py:379
  263.2 5.8 %copy.32 = f32[4,2,64,16,64]{2,3,4,1,0:T(8,128)} copy(f32[4,2,64,16,64]{4,3,2,1,0:T(8,128)} %reshape.818) | data formatting | bytes 4194304 | tf_op jit(solution)/shard_map/reshape | solution.py:379
  269.1 3.5 reshape.819
  272.6 3.2 fusion.63
  275.8 1.3 slice_reduce_fusion.1
  277.1 1.2 broadcast_in_dim.55.refs_1_
  278.4 29.9 %exchange4.1 = (f32[8,64,1024]{2,1,0:T(8,128)}, f32[8,8,128]{2,1,0:T(8,128)}) custom-call(f32[8,64,1024]{2,1,0:T(8,128)} %bitcast.67, f32[8,8,128]{2,1,0:T(8,128)} %broadcast_in_dim.55.refs_1_), custom_call_target="tpu_custom_call" | custom-call | tf_op jit(solution)/shard_map/exchange4/pallas_call | solution.py:291
  308.3 4.5 %reshape.821 = f32[8,2,32,16,64]{4,3,2,1,0:T(8,128)} reshape(f32[8,64,1024]{2,1,0:T(8,128)} %get-tuple-element.32) | data formatting | bytes 4194304 | tf_op jit(solution)/shard_map/reshape | solution.py:390
  312.8 6.9 %copy.33 = f32[8,2,32,16,64]{2,4,3,1,0:T(8,128)} copy(f32[8,2,32,16,64]{4,3,2,1,0:T(8,128)} %reshape.821) | data formatting | bytes 4194304 | tf_op jit(solution)/shard_map/reshape | solution.py:390
  319.8 7.5 %reshape.822 = f32[256,2048]{1,0:T(8,128)} reshape(f32[8,2,16,64,32]{4,3,2,1,0:T(8,128)} %bitcast.50) | data formatting | bytes 4194304 | tf_op jit(solution)/shard_map/reshape | solution.py:391
  327.3 3.4 fusion.64
  330.7 2.4 collective-permute-start.2
  333.2 3.8 collective-permute-done.2.up_ref
  337.6 1.4 slice_reduce_fusion
  339.6 3.0 collective-permute-done.3
  343.6 50.6 %interp.1 = f32[3,128,256]{2,1,0:T(8,128)} custom-call(s32[2,128,256]{2,1,0:T(8,128)} %bitcast.73, s32[128,256]{1,0:T(8,128)} %reshape.805.z_ref, f32[3,128,256]{2,1,0:T(8,128)} %bitcast.71, f32[128,256]{1,0:T(8,128)} %compare_select_fusion.2.q_ref, f32[64,32,256]{2,1,0:T(8,128)} %bitcast.59, f32[5,32,256]{2,1,0:T(8,128)} %copy-done.5, ...), custom_call_target="tpu_custom_call" | custom-call | tf_op jit(solution)/shard_map/interp/pallas_call | solution.py:427
  394.2 2.1 copy.40
  (54 shorter events, 10.8 us)
Async XLA Ops:
  0.6 5.6 %copy-start.6 = (s32[32768]{0:T(1024)S(1)}, s32[32768]{0:T(1024)}, u32[]{:S(2)}) copy-start(s32[32768]{0:T(1024)} %param.15) | copy-start | bytes 393220
  42.0 8.6 %collective-permute-start = (f32[69,5,256]{2,0,1:T(8,128)S(1)}, f32[69,5,256]{2,0,1:T(8,128)S(1)}, u32[]{:S(2)}, u32[]{:S(2)}) collective-permute-start(f32[69,5,256]{2,0,1:T(8,128)S(1)} %copy.27), channel_id=1, source_target_pairs={{7,0},{0,1},{1,2},{2,3},{3,4},{4,5},{5,6},{6,7},{15,8},{8,9},{9,10... | collective-permute-start | bytes 1059848 | tf_op jit(solution)/shard_map/ppermute | solution.py:25
  57.6 7.9 %collective-permute-start.1 = (f32[5,32,256]{2,1,0:T(8,128)S(1)}, f32[5,32,256]{2,1,0:T(8,128)S(1)}, u32[]{:S(2)}, u32[]{:S(2)}) collective-permute-start(f32[5,32,256]{2,1,0:T(8,128)S(1)} %slice.164), channel_id=1, source_target_pairs={{24,0},{0,8},{8,16},{16,24},{25,1},{1,9},{9,17},{17,25},{26,2},{2,... | collective-permute-start | bytes 491528 | tf_op jit(solution)/shard_map/ppermute | solution.py:25
  60.3 5.1 %copy-start.4 = (f32[256,256]{1,0:T(8,128)S(1)}, f32[256,256]{1,0:T(8,128)}, u32[]{:S(2)}) copy-start(f32[256,256]{1,0:T(8,128)} %constant.269.clone) | copy-start | bytes 786436
  83.1 27.9 %copy-start.1 = (f32[512,512]{1,0:T(8,128)S(1)}, f32[512,512]{1,0:T(8,128)}, u32[]{:S(2)}) copy-start(f32[512,512]{1,0:T(8,128)} %constant.270.clone) | copy-start | bytes 3145732
  186.2 1.2 copy-start.2
  319.8 7.5 %copy-start.3 = (f32[256,256]{1,0:T(8,128)S(1)}, f32[256,256]{1,0:T(8,128)}, u32[]{:S(2)}) copy-start(f32[256,256]{1,0:T(8,128)} %constant.273.clone) | copy-start | bytes 786436
  330.7 12.0 %copy-start = (f32[2048,256]{1,0:T(8,128)}, f32[2048,256]{1,0:T(8,128)S(1)}, u32[]{:S(2)}) copy-start(f32[2048,256]{1,0:T(8,128)S(1)} %fusion.64) | copy-start | bytes 6291460
  330.7 6.2 %collective-permute-start.2 = (f32[5,32,256]{2,1,0:T(8,128)S(1)}, f32[5,32,256]{2,1,0:T(8,128)S(1)}, u32[]{:S(2)}, u32[]{:S(2)}) collective-permute-start(f32[5,32,256]{2,1,0:T(8,128)S(1)} %bitcast.79), channel_id=1, source_target_pairs={{8,0},{16,8},{24,16},{0,24},{9,1},{17,9},{25,17},{1,25},{10,2},{18... | collective-permute-start | bytes 491528 | tf_op jit(solution)/shard_map/ppermute | solution.py:25
  337.0 6.6 %copy-start.5 = (f32[5,32,256]{2,1,0:T(8,128)}, f32[5,32,256]{2,1,0:T(8,128)S(1)}, u32[]{:S(2)}) copy-start(f32[5,32,256]{2,1,0:T(8,128)S(1)} %collective-permute-done.2.up_ref) | copy-start | bytes 491524
  337.2 5.4 %collective-permute-start.3 = (f32[69,5,256]{2,0,1:T(8,128)S(1)}, f32[69,5,256]{2,0,1:T(8,128)S(1)}, u32[]{:S(2)}, u32[]{:S(2)}) collective-permute-start(f32[69,5,256]{2,0,1:T(8,128)S(1)} %copy.34), channel_id=1, source_target_pairs={{1,0},{2,1},{3,2},{4,3},{5,4},{6,5},{7,6},{0,7},{9,8},{10,9},{11,1... | collective-permute-start | bytes 1059848 | tf_op jit(solution)/shard_map/ppermute | solution.py:25
